TPU v7x, 32 devices: a whole 2x2x4 slice. The times are simulated.
32 devices in a mesh: ep: 16 (over z, y, core), rep: 2 (over x).
Axes of the slice: x: 2, y: 2, z: 4, core: 2. Of those that a mesh axis runs over, the one named last changes fastest.
Arguments:
- out_grad: bfloat16 [4096, 2048], P(('ep', 'rep')), may hold values from -6 to 6
- hidden: bfloat16 [4096, 8, 768], P(('ep', 'rep')), may hold values from -6 to 6
- expert_ids: int32 [4096, 8], P(('ep', 'rep')), may hold values from 0 to 15, all different within a row; in each aligned block of 128 rows (0 to 127, 128 to 255, ...) at most 72 rows name the same one
- gates: float32 [4096, 8], P(('ep', 'rep')), may hold values from 0.02 to 0.5
- weights: bfloat16 [16, 768, 2048], P('ep', 'rep'), may hold values from -0.125 to 0.125
- row_moment: float32 [16, 768], P('ep', 'rep'), may hold values from 16 to 1024
- col_moment: float32 [16, 2, 2048], P('ep', 'rep'), may hold values from 16 to 1024
Outputs:
- hidden_grad: bfloat16 [4096, 8, 768], P(('ep', 'rep'))
- update: bfloat16 [16, 768, 2048], P('ep', 'rep')
- row_new: float32 [16, 768], P('ep', 'rep')
- col_new: float32 [16, 2, 2048], P('ep', 'rep')
Inputs may be any that keep to these rules, and one draw needn't show every extreme that they name: `expert_ids`: the 8 experts of a token are distinct. Among the tokens of one device no expert is chosen more than 72 times, and in every draw some device reaches 72 for some expert.
All inputs are finite; a program needn't handle non-finite values.
Results may differ from a plain program's by a relative error of at most 0.014.
Values may be sent and summed in bfloat16 or wider, within the bound.
A program may use at most 128 MiB of HBM per device.

v0:
```python
import functools

import jax
import jax.numpy as jnp
from jax import lax
from jax.experimental import pallas as pl
from jax.experimental.pallas import tpu as pltpu
from jax.sharding import PartitionSpec as P

decay_rate = 0.9
epsilon = 1e-06
MESH = pl.DeviceIdType.MESH


def up_to(value, step):
    return -(-value // step) * step


def kernel(
    dims,
    og_ref,
    hidden_ref,
    ids_ref,
    gates_ref,
    w_ref,
    rowm_ref,
    colm_ref,
    returned_ref,
    out_ref,
    update_ref,
    rown_ref,
    coln_ref,
    og_all,
    hid,
    slot,
    table,
    place_all,
    hsend,
    hrecv,
    rows,
    igbuf,
    wfull,
    parts,
    grad,
    og_recv,
    up_sem,
    down_sem,
    y_sem,
    core_sem,
    pl_send,
    pl_recv,
    h_send,
    h_recv,
    r_send,
    r_recv,
    w_send,
    w_recv,
    g_send,
    g_recv,
    l_sem,
):
    n_ep, n_rep, outer, sent, cap, chunks = dims
    tok, width = og_ref.shape
    routes, inner = hidden_ref.shape
    top = routes // tok
    own_rows = inner // n_rep
    wide = width // chunks
    term = wfull
    me = lax.axis_index("ep")
    rep = lax.axis_index("rep")
    z, y, c = me // 4, (me // 2) % 2, me % 2
    y_dev = z * 4 + (1 - y) * 2 + c
    c_dev = z * 4 + y * 2 + (1 - c)
    way = 1 - 2 * (z // (outer // 2))

    barrier = pltpu.get_barrier_semaphore()
    for d in range(1, n_ep):
        pl.semaphore_signal(
            barrier, inc=1, device_id={"ep": lax.rem(me + d, n_ep)}, device_id_type=MESH
        )
    for d in range(1, n_rep):
        pl.semaphore_signal(
            barrier, inc=1, device_id={"rep": lax.rem(rep + d, n_rep)}, device_id_type=MESH
        )
    pl.semaphore_wait(barrier, n_ep - 1 + n_rep - 1)

    def remote(src, dst, send, recv, **where):
        return pltpu.make_async_remote_copy(
            src_ref=src, dst_ref=dst, send_sem=send, recv_sem=recv,
            device_id=where, device_id_type=MESH,
        )

    def og_copy(block, send, to, own):
        src = og_ref if own else og_all.at[block]
        return remote(src, og_all.at[block], send, og_recv.at[block], ep=to)

    def og_wait(block):
        remote(og_all.at[block], og_all.at[block], up_sem.at[0], og_recv.at[block], ep=me).wait_recv()

    def fan(zs, k, act):
        block = zs * 4 + y * 2 + c
        act(og_copy(block, y_sem.at[zs], y_dev, k == 0))
        act(og_copy(block, core_sem.at[zs * 2], c_dev, k == 0))

    def rise(zs, k, act):
        block = zs * 4 + y * 2 + c

        @pl.when(z + 1 < outer)
        def _():
            act(og_copy(block, up_sem.at[zs], me + 4, k == 0))

    def sink(zs, k, act):
        block = zs * 4 + y * 2 + c

        @pl.when(z > 0)
        def _():
            act(og_copy(block, down_sem.at[zs], me - 4, k == 0))

    def cross(zs, act):
        block = zs * 4 + (1 - y) * 2 + c
        act(og_copy(block, core_sem.at[zs * 2 + 1], c_dev, False))

    start = lambda copy: copy.start()
    finish = lambda copy: copy.wait_send()

    def own_sends(act):
        rise(z, 0, act)
        sink(z, 0, act)
        fan(z, 0, act)

    def forward(k, act, arrive):
        low, high = z - k, z + k

        @pl.when(low >= 0)
        def _():
            if arrive:
                og_wait(low * 4 + y * 2 + c)
            rise(low, k, act)
            fan(low, k, act)

        @pl.when(high < outer)
        def _():
            if arrive:
                og_wait(high * 4 + y * 2 + c)
            sink(high, k, act)
            fan(high, k, act)

    def crossing(k, act, arrive):
        for zs, ok in ((z - k, z - k >= 0), (z + k, z + k < outer))[: 1 if k == 0 else 2]:

            @pl.when(ok)
            def _():
                if arrive:
                    og_wait(zs * 4 + (1 - y) * 2 + c)
                cross(zs, act)

    own_sends(start)
    own_og = pltpu.make_async_copy(og_ref, og_all.at[me], l_sem.at[0])
    own_w = pltpu.make_async_copy(w_ref, wfull.at[rep], l_sem.at[1])
    own_hidden = pltpu.make_async_copy(hidden_ref, hid, l_sem.at[2])
    own_hidden.start()
    own_og.start()
    own_w.start()
    w_copies = []
    for d in range(1, n_rep):
        q = lax.rem(rep + d, n_rep)
        w_copies.append(remote(w_ref, wfull.at[rep], w_send.at[d], w_recv.at[rep], rep=q))
        w_copies[-1].start()

    experts = lax.broadcasted_iota(jnp.int32, (tok, up_to(n_ep, 128)), 1)
    chosen = jnp.zeros(experts.shape, jnp.float32)
    gate = jnp.zeros(experts.shape, jnp.float32)
    for k in range(top):
        named = experts == ids_ref[:, k : k + 1]
        chosen = jnp.where(named, 1.0, chosen)
        gate = jnp.where(named, gates_ref[:, k : k + 1], gate)
    row_i = lax.broadcasted_iota(jnp.int32, (tok, tok), 0)
    col_i = lax.broadcasted_iota(jnp.int32, (tok, tok), 1)
    earlier = jnp.where(row_i < col_i, 1.0, 0.0).astype(jnp.bfloat16)
    rank = lax.dot_general(
        chosen.T.astype(jnp.bfloat16), earlier, (((1,), (0,)), ((), ())),
        preferred_element_type=jnp.float32,
    )
    place = jnp.where(chosen.T > 0.5, rank, -1.0)[:n_ep]
    gate = gate.T[:n_ep]
    first_row = lax.broadcasted_iota(jnp.int32, (n_ep, 8, tok), 1) == 0
    table[...] = jnp.where(first_row, place[:, None, :], gate[:, None, :])
    place_all[me] = table[me]
    if cap > sent:
        hrecv[:, sent:, :] = jnp.zeros((n_ep, cap - sent, inner), jnp.bfloat16)

    spread = jnp.where(
        lax.broadcasted_iota(jnp.int32, (tok, routes), 1) // top
        == lax.broadcasted_iota(jnp.int32, (tok, routes), 0), 1.0, 0.0,
    ).astype(jnp.bfloat16)
    named = lax.dot_general(
        ids_ref[...].astype(jnp.float32).astype(jnp.bfloat16), spread, (((0,), (0,)), ((), ())),
        preferred_element_type=jnp.float32,
    )
    turn = lax.broadcasted_iota(jnp.int32, (top, routes), 1) % top
    mine = turn == lax.broadcasted_iota(jnp.int32, (top, routes), 0)
    named = jnp.sum(jnp.where(mine, named, 0.0), axis=0, keepdims=True)
    ranks = jnp.dot(place.astype(jnp.bfloat16), spread, preferred_element_type=jnp.float32)
    number = lax.broadcasted_iota(jnp.int32, (n_ep, routes), 0).astype(jnp.float32)
    slot[...] = jnp.sum(
        jnp.where(named == number, ranks + number * cap, 0.0), axis=0, keepdims=True
    )

    def place_copy(d):
        e = lax.rem(me + d, n_ep)
        return remote(table.at[e], place_all.at[me], pl_send.at[d], pl_recv.at[me], ep=e)

    @pl.loop(1, n_ep)
    def _(d):
        place_copy(d).start()

    def h_copy(e):
        return remote(hsend.at[e, pl.ds(0, sent)], hrecv.at[me, pl.ds(0, sent)], h_send.at[e], h_recv.at[me], ep=e)

    def r_copy(s):
        return remote(igbuf.at[s, pl.ds(0, sent)], returned_ref.at[me], r_send.at[s], r_recv.at[me], ep=s)

    def plane(k):
        return lax.rem(z + way * k + outer, outer)

    def slot_pick(first):
        ids = lax.broadcasted_iota(jnp.int32, (4 * cap, routes), 0) + first * cap
        return jnp.where(ids.astype(jnp.float32) == slot[...], 1.0, 0.0).astype(jnp.bfloat16)

    def hidden_group(k):
        first = plane(k) * 4
        got = jnp.dot(slot_pick(first), hid[...], preferred_element_type=jnp.float32)
        hsend[pl.ds(first, 4)] = got.astype(jnp.bfloat16).reshape(4, cap, inner)

        @pl.loop(0, 4)
        def _(i):
            e = first + i

            @pl.when(e != me)
            def _():
                h_copy(e).start()

            @pl.when(e == me)
            def _():
                hrecv[me] = hsend[me]

    own_hidden.wait()
    hidden_group(0)
    for k in range(1, outer):
        forward(k, start, True)
        hidden_group(k)
        crossing(k - 1, start, True)
    crossing(outer - 1, start, True)

    for d in range(1, n_rep):
        q = lax.rem(rep + d, n_rep)
        remote(w_ref, wfull.at[q], w_send.at[d], w_recv.at[q], rep=q).wait_recv()

    @pl.loop(1, n_ep)
    def _(d):
        s = lax.rem(me + d, n_ep)
        remote(table.at[s], place_all.at[s], pl_send.at[d], pl_recv.at[s], ep=s).wait_recv()

    own_og.wait()
    own_w.wait()

    @pl.loop(0, outer)
    def _(k):
        first = plane(k) * 4
        og_wait(first + 1 - c)
        og_wait(first + 3 - c)

        @pl.loop(0, 4)
        def _(i):
            s = first + i
            info = place_all[s]
            ids = lax.broadcasted_iota(jnp.int32, (cap, tok), 0).astype(jnp.float32)
            pick = jnp.where(ids == info[0:1, :], 1.0, 0.0)
            factor = jnp.sum(pick * info[1:2, :], axis=1, keepdims=True)
            got = factor * jnp.dot(
                pick.astype(jnp.bfloat16), og_all[s], preferred_element_type=jnp.float32
            )
            rows[pl.ds(pl.multiple_of(s * cap, 16), cap), :] = got.astype(jnp.bfloat16)

        here = rows[pl.ds(pl.multiple_of(first * cap, 16), 4 * cap), :]
        back = lax.dot_general(
            here,
            wfull[...].reshape(inner, width),
            (((1,), (1,)), ((), ())),
            preferred_element_type=jnp.float32,
        )
        igbuf[pl.ds(first, 4)] = back.astype(jnp.bfloat16).reshape(4, cap, inner)

        @pl.loop(0, 4)
        def _(i):
            s = first + i

            @pl.when(s != me)
            def _():
                r_copy(s).start()

    own = pltpu.make_async_copy(igbuf.at[me, pl.ds(0, sent)], returned_ref.at[me], r_recv.at[me])
    own.start()

    @pl.loop(1, n_ep)
    def _(d):
        s = lax.rem(me + d, n_ep)
        remote(hsend.at[s, pl.ds(0, sent)], hrecv.at[s, pl.ds(0, sent)], h_send.at[s], h_recv.at[s], ep=s).wait_recv()

    def g_copy(d, j, q, slot):
        cols = pl.ds(j * wide, wide)
        return remote(
            term.at[q, :, cols], parts.at[slot, :, cols],
            g_send.at[d, j], g_recv.at[slot, j], rep=q,
        )

    left = hrecv[...].reshape(n_ep * cap, inner)
    for j in range(chunks):
        cols = pl.ds(j * wide, wide)
        got = lax.dot_general(
            left, rows[:, cols], (((0,), (0,)), ((), ())), preferred_element_type=jnp.float32
        )
        term[:, :, cols] = got.astype(jnp.bfloat16).reshape(n_rep, own_rows, wide)
        for d in range(1, n_rep):
            g_copy(d, j, lax.rem(rep + d, n_rep), rep).start()

    def back_copy(first):
        return pltpu.make_async_copy(
            returned_ref.at[pl.ds(first, 4)], hsend.at[pl.ds(first, 4), pl.ds(0, sent)], l_sem.at[0]
        )

    def collect(k):
        first = plane(k) * 4

        @pl.loop(0, 4)
        def _(i):
            s = first + i

            @pl.when(s != me)
            def _():
                h_copy(s).wait_send()
                remote(
                    igbuf.at[s, pl.ds(0, sent)], returned_ref.at[s], r_send.at[s], r_recv.at[s], ep=s
                ).wait_recv()

        back_copy(first).start()
        back_copy(first).wait()
        got = lax.dot_general(
            slot_pick(first),
            hsend[pl.ds(first, 4)].reshape(4 * cap, inner),
            (((0,), (0,)), ((), ())),
            preferred_element_type=jnp.float32,
        ).astype(jnp.bfloat16)
        out_ref[...] = got if k == 0 else out_ref[...] + got

    own.wait()
    for k in range(outer - 1):
        collect(k)

    total = jnp.zeros((own_rows, 1), jnp.float32)
    for j in range(chunks):
        cols = pl.ds(j * wide, wide)
        part = term[rep, :, cols].astype(jnp.float32)
        for d in range(1, n_rep):
            q = lax.rem(rep + d, n_rep)
            g_copy(d, j, q, q).wait_recv()
            part = part + parts[q, :, cols].astype(jnp.float32)
        grad[:, cols] = part
        square = part * part
        total = total + jnp.sum(square, axis=1, keepdims=True)
        coln_ref[:, cols] = decay_rate * colm_ref[:, cols] + (1.0 - decay_rate) * (
            jnp.sum(square, axis=0, keepdims=True) / own_rows + epsilon
        )
    diagonal = lax.broadcasted_iota(jnp.int32, (own_rows, own_rows), 0) == (
        lax.broadcasted_iota(jnp.int32, (own_rows, own_rows), 1)
    )
    rowm = jnp.sum(jnp.where(diagonal, rowm_ref[...], 0.0), axis=1, keepdims=True)
    row_new = decay_rate * rowm + (1.0 - decay_rate) * (total / width + epsilon)
    rown_ref[...] = jnp.sum(jnp.where(diagonal, row_new, 0.0), axis=0, keepdims=True)
    mean = jnp.sum(row_new, axis=0, keepdims=True) / own_rows
    for j in range(chunks):
        cols = pl.ds(j * wide, wide)
        second = row_new * coln_ref[:, cols] / mean
        update_ref[:, cols] = (grad[:, cols] * lax.rsqrt(second)).astype(jnp.bfloat16)

    collect(outer - 1)

    @pl.loop(1, n_ep)
    def _(d):
        s = lax.rem(me + d, n_ep)
        place_copy(d).wait_send()
        r_copy(s).wait_send()

    own_sends(finish)
    for k in range(1, outer):
        forward(k, finish, False)
        crossing(k - 1, finish, False)
    crossing(outer - 1, finish, False)
    for copy in w_copies:
        copy.wait_send()
    for j in range(chunks):
        for d in range(1, n_rep):
            g_copy(d, j, lax.rem(rep + d, n_rep), rep).wait_send()


def local(out_grad, hidden, expert_ids, gates, weights, row_moment, col_moment):
    tok, top = expert_ids.shape
    width = out_grad.shape[1]
    inner = hidden.shape[2]
    n_ep, n_rep = lax.axis_size("ep"), lax.axis_size("rep")
    capacity = max(2, tok * top * 9 // (8 * n_ep))
    sent, cap = up_to(capacity, 8), up_to(capacity, 16)
    outer = n_ep // 4
    own_rows = inner // n_rep
    routes = tok * top
    chunks = 4

    vmem = pl.BlockSpec(memory_space=pltpu.VMEM)
    anywhere = pl.BlockSpec(memory_space=pl.ANY)
    dma = pltpu.SemaphoreType.DMA
    _, hidden_grad, update, row_new, col_new = pl.pallas_call(
        functools.partial(kernel, (n_ep, n_rep, outer, sent, cap, chunks)),
        out_shape=(
            jax.ShapeDtypeStruct((n_ep, sent, inner), jnp.bfloat16),
            jax.ShapeDtypeStruct((routes, inner), jnp.bfloat16),
            jax.ShapeDtypeStruct((own_rows, width), jnp.bfloat16),
            jax.ShapeDtypeStruct((1, own_rows), jnp.float32),
            jax.ShapeDtypeStruct((1, width), jnp.float32),
        ),
        in_specs=[anywhere, anywhere, vmem, vmem, anywhere, vmem, vmem],
        out_specs=(anywhere, vmem, vmem, vmem, vmem),
        scratch_shapes=[
            pltpu.VMEM((n_ep, tok, width), jnp.bfloat16),
            pltpu.VMEM((routes, inner), jnp.bfloat16),
            pltpu.VMEM((1, routes), jnp.float32),
            pltpu.VMEM((n_ep, 8, tok), jnp.float32),
            pltpu.VMEM((n_ep, 8, tok), jnp.float32),
            pltpu.VMEM((n_ep, cap, inner), jnp.bfloat16),
            pltpu.VMEM((n_ep, cap, inner), jnp.bfloat16),
            pltpu.VMEM((n_ep * cap, width), jnp.bfloat16),
            pltpu.VMEM((n_ep, cap, inner), jnp.bfloat16),
            pltpu.VMEM((n_rep, own_rows, width), jnp.bfloat16),
            pltpu.VMEM((n_rep, own_rows, width), jnp.bfloat16),
            pltpu.VMEM((own_rows, width), jnp.float32),
            dma((n_ep,)),
            dma((outer,)),
            dma((outer,)),
            dma((outer,)),
            dma((2 * outer,)),
            dma((n_ep,)),
            dma((n_ep,)),
            dma((n_ep,)),
            dma((n_ep,)),
            dma((n_ep,)),
            dma((n_ep,)),
            dma((n_rep,)),
            dma((n_rep,)),
            dma((n_rep, chunks)),
            dma((n_rep, chunks)),
            dma((3,)),
        ],
        compiler_params=pltpu.CompilerParams(
            collective_id=0, has_side_effects=True, vmem_limit_bytes=67043328
        ),
    )(
        out_grad,
        hidden.reshape(routes, inner),
        expert_ids,
        gates,
        weights[0],
        row_moment.reshape(1, own_rows),
        col_moment.reshape(1, width),
    )

    return (
        hidden_grad.reshape(tok, top, inner),
        update[None],
        row_new.reshape(1, own_rows),
        col_new.reshape(1, 1, width),
    )


def solution(mesh):
    return jax.shard_map(
        local,
        mesh=mesh,
        in_specs=(
            P(("ep", "rep"), None),
            P(("ep", "rep"), None, None),
            P(("ep", "rep"), None),
            P(("ep", "rep"), None),
            P("ep", "rep", None),
            P("ep", "rep"),
            P("ep", "rep", None),
        ),
        out_specs=(
            P(("ep", "rep"), None, None),
            P("ep", "rep", None),
            P("ep", "rep"),
            P("ep", "rep", None),
        ),
        check_vma=False,
    )
```

profile of v0, /device:TPU:29, one launch (start us, length us, event | category | flops | bytes accessed | tf_op | source)
XLA Modules:
  0.0 136.9 jit_solution(10673418931601055241)
XLA Ops:
  0.6 1.4 %copy.11.ids_ref = s32[128,8]{1,0:T(8,128)} copy(s32[128,8]{0,1:T(8,128)} %param.9) | data formatting | bytes 8192 | tf_op args[2]
  2.0 1.4 %copy.12.gates_ref = f32[128,8]{1,0:T(8,128)} copy(f32[128,8]{0,1:T(8,128)} %param.10) | data formatting | bytes 8192 | tf_op args[3]
  3.5 128.3 %shard_map.102 = (bf16[16,72,768]{2,1,0:T(8,128)(2,1)}, bf16[1024,768]{1,0:T(8,128)(2,1)}, bf16[384,2048]{1,0:T(8,128)(2,1)}, f32[1,384]{1,0:T(1,128)}, f32[1,2048]{1,0:T(1,128)}) custom-call(bf16[128,2048]{1,0:T(8,128)(2,1)} %og_ref.1, bf16[1024,768]{1,0:T(8,128)(2,1)} %bitcast.6, s32[128,8]{1,0:T(8,128)} %copy.11.ids_ref, f32[128,8]{1,0:T(8,128)} %copy.12.gates_ref, ...), custom_call_target="tpu_custom_call" | custom-call | tf_op jit(solution)/shard_map/pallas_call | solution.py:421
  131.8 0.0 copy-start
  131.8 2.8 %copy.17 = bf16[128,8,768]{2,1,0:T(8,128)(2,1)} copy(bf16[128,8,768]{2,1,0:T(8,128)(2,1)} %bitcast.9) | data formatting | bytes 3145728
  134.6 0.0 copy-done
  134.6 0.0 copy-start.2
  134.6 0.0 copy-start.1
  134.6 1.1 copy.18
  135.7 0.0 copy-done.2
  135.7 0.6 copy.19
  136.3 0.0 copy-done.1
  136.3 0.6 copy.20
Async XLA Ops:
  131.8 2.8 %copy-start = (bf16[384,2048]{1,0:T(8,128)(2,1)S(1)}, bf16[384,2048]{1,0:T(8,128)(2,1)}, u32[]{:S(2)}) copy-start(bf16[384,2048]{1,0:T(8,128)(2,1)} %get-tuple-element.9) | copy-start | bytes 4718596
  134.6 1.1 copy-start.2
  134.6 1.7 %copy-start.1 = (f32[1,2048]{1,0:T(1,128)S(1)}, f32[1,2048]{1,0:T(1,128)}, u32[]{:S(2)}) copy-start(f32[1,2048]{1,0:T(1,128)} %get-tuple-element.11) | copy-start | bytes 24580
where the time goes:
time: 137 us
  Pallas kernels  128 us (93%)
  local copies, waits for them, and re-layouts  7.92 us (6%)
    pallas_call x1, Pallas kernels, local(): pl.pallas_call(functools.partial(kernel, (n_ep, n_rep, outer, sent, cap,...  128 us
    unnamed x12, local copies, waits for them, and re-layouts  7.92 us

commit v1 on v0

v1 whole, which is shorter than its diff:
```python
import functools

import jax
import jax.numpy as jnp
from jax import lax
from jax.experimental import pallas as pl
from jax.experimental.pallas import tpu as pltpu
from jax.sharding import PartitionSpec as P

decay_rate = 0.9
epsilon = 1e-06
MESH = pl.DeviceIdType.MESH
scope = jax.named_scope


def up_to(value, step):
    return -(-value // step) * step


def kernel(
    dims,
    og_ref,
    hidden_ref,
    ids_ref,
    gates_ref,
    w_ref,
    rowm_ref,
    colm_ref,
    out_ref,
    update_ref,
    rown_ref,
    coln_ref,
    og_all,
    slot,
    table,
    place_all,
    hsend,
    hrecv,
    rows,
    igbuf,
    back,
    wfull,
    parts,
    grad,
    og_recv,
    own_sem,
    relay_sem,
    y_sem,
    core_sem,
    pl_send,
    pl_recv,
    h_send,
    h_recv,
    r_send,
    r_recv,
    w_send,
    w_recv,
    g_send,
    g_recv,
    l_sem,
):
    n_ep, n_rep, outer, sent, cap, chunks = dims
    tok, width = og_ref.shape
    routes, inner = hidden_ref.shape
    top = routes // tok
    own_rows = inner // n_rep
    wide = width // chunks
    term = wfull
    me = lax.axis_index("ep")
    rep = lax.axis_index("rep")
    z, y, c = me // 4, (me // 2) % 2, me % 2
    y_dev = z * 4 + (1 - y) * 2 + c
    c_dev = z * 4 + y * 2 + (1 - c)
    half = outer // 2
    low = z < half
    near = jnp.where(low, z, outer - 1 - z)
    gateway = near == half - 1

    def real(p):
        return jnp.where(low, p, outer - 1 - p)

    def spot(k):
        return lax.rem(near + k, outer)

    def plane(k):
        return real(spot(k))

    barrier = pltpu.get_barrier_semaphore()
    for d in range(1, n_ep):
        pl.semaphore_signal(
            barrier, inc=1, device_id={"ep": lax.rem(me + d, n_ep)}, device_id_type=MESH
        )
    for d in range(1, n_rep):
        pl.semaphore_signal(
            barrier, inc=1, device_id={"rep": lax.rem(rep + d, n_rep)}, device_id_type=MESH
        )
    with scope("entry"):
        pl.semaphore_wait(barrier, n_ep - 1 + n_rep - 1)

    def remote(src, dst, send, recv, **where):
        return pltpu.make_async_remote_copy(
            src_ref=src, dst_ref=dst, send_sem=send, recv_sem=recv,
            device_id=where, device_id_type=MESH,
        )

    def og_copy(block, send, to, own):
        src = og_ref if own else og_all.at[block]
        return remote(src, og_all.at[block], send, og_recv.at[block], ep=to)

    def og_wait(block):
        remote(og_all.at[block], og_all.at[block], own_sem.at[0], og_recv.at[block], ep=me).wait_recv()

    def column(p):
        return real(p) * 4 + y * 2 + c

    def fan(zs, own, act):
        block = zs * 4 + y * 2 + c
        act(og_copy(block, y_sem.at[zs], y_dev, own))
        act(og_copy(block, core_sem.at[zs * 2], c_dev, own))

    start = lambda copy: copy.start()
    finish = lambda copy: copy.wait_send()

    def own_sends(act):
        for t in range(1, half):
            act(og_copy(me, own_sem.at[t], column(lax.rem(near + t, half)), True))
        fan(z, True, act)

    def own_across(act):
        act(og_copy(me, own_sem.at[0], column(half), True))

    def relay(k, act, arrive):
        block = column(spot(k))
        if arrive:
            og_wait(block)

        @pl.when(gateway & (spot(k) >= half))
        def _():
            for t in range(1, half):
                sem = relay_sem.at[k * half + t]
                act(og_copy(block, sem, column(lax.rem(near + t, half)), False))

        fan(plane(k), False, act)

    def crossing(k, act, arrive):
        zs = plane(k)
        block = zs * 4 + (1 - y) * 2 + c
        if arrive:
            og_wait(block)
        act(og_copy(block, core_sem.at[zs * 2 + 1], c_dev, False))

    own_sends(start)

    @pl.when(gateway)
    def _():
        own_across(start)

    own_og = pltpu.make_async_copy(og_ref, og_all.at[me], l_sem.at[0])
    own_w = pltpu.make_async_copy(w_ref, wfull.at[rep], l_sem.at[1])
    own_hidden = pltpu.make_async_copy(hidden_ref, out_ref, l_sem.at[2])
    own_hidden.start()
    own_og.start()
    own_w.start()
    w_copies = []
    for d in range(1, n_rep):
        q = lax.rem(rep + d, n_rep)
        w_copies.append(remote(w_ref, wfull.at[rep], w_send.at[d], w_recv.at[rep], rep=q))
        w_copies[-1].start()

    experts = lax.broadcasted_iota(jnp.int32, (n_ep, tok), 0)
    chosen = jnp.zeros(experts.shape, jnp.float32)
    gate = jnp.zeros(experts.shape, jnp.float32)
    for k in range(top):
        named = experts == ids_ref[k : k + 1, :]
        chosen = jnp.where(named, 1.0, chosen)
        gate = jnp.where(named, gates_ref[k : k + 1, :], gate)
    row_i = lax.broadcasted_iota(jnp.int32, (tok, tok), 0)
    col_i = lax.broadcasted_iota(jnp.int32, (tok, tok), 1)
    earlier = jnp.where(row_i < col_i, 1.0, 0.0).astype(jnp.bfloat16)
    rank = jnp.dot(chosen.astype(jnp.bfloat16), earlier, preferred_element_type=jnp.float32)
    place = jnp.where(chosen > 0.5, rank, -1.0)
    first_row = lax.broadcasted_iota(jnp.int32, (n_ep, 8, tok), 1) == 0
    table[...] = jnp.where(first_row, place[:, None, :], gate[:, None, :])
    place_all[me] = table[me]
    if cap > sent:
        hrecv[:, sent:, :] = jnp.zeros((n_ep, cap - sent, inner), jnp.bfloat16)
        back[:, sent:, :] = jnp.zeros((n_ep, cap - sent, inner), jnp.bfloat16)

    spread = jnp.where(
        lax.broadcasted_iota(jnp.int32, (tok, routes), 1) // top
        == lax.broadcasted_iota(jnp.int32, (tok, routes), 0), 1.0, 0.0,
    ).astype(jnp.bfloat16)
    named = jnp.dot(
        ids_ref[...].astype(jnp.float32).astype(jnp.bfloat16), spread,
        preferred_element_type=jnp.float32,
    )
    turn = lax.broadcasted_iota(jnp.int32, (top, routes), 1) % top
    mine = turn == lax.broadcasted_iota(jnp.int32, (top, routes), 0)
    named = jnp.sum(jnp.where(mine, named, 0.0), axis=0, keepdims=True)
    ranks = jnp.dot(place.astype(jnp.bfloat16), spread, preferred_element_type=jnp.float32)
    number = lax.broadcasted_iota(jnp.int32, (n_ep, routes), 0).astype(jnp.float32)
    slot[...] = jnp.sum(
        jnp.where(named == number, ranks + number * cap, 0.0), axis=0, keepdims=True
    )

    def place_copy(d):
        e = lax.rem(me + d, n_ep)
        return remote(table.at[e], place_all.at[me], pl_send.at[d], pl_recv.at[me], ep=e)

    @pl.loop(1, n_ep)
    def _(d):
        place_copy(d).start()

    def h_copy(e):
        return remote(hsend.at[e, pl.ds(0, sent)], hrecv.at[me, pl.ds(0, sent)], h_send.at[e], h_recv.at[me], ep=e)

    def r_copy(s):
        return remote(igbuf.at[s, pl.ds(0, sent)], back.at[me, pl.ds(0, sent)], r_send.at[s], r_recv.at[me], ep=s)

    def slot_pick(first):
        ids = lax.broadcasted_iota(jnp.int32, (4 * cap, routes), 0) + first * cap
        return jnp.where(ids.astype(jnp.float32) == slot[...], 1.0, 0.0).astype(jnp.bfloat16)

    def hidden_group(k):
        first = plane(k) * 4
        got = jnp.dot(slot_pick(first), out_ref[...], preferred_element_type=jnp.float32)
        hsend[pl.ds(first, 4)] = got.astype(jnp.bfloat16).reshape(4, cap, inner)
        if k == 0:
            hrecv[me] = hsend[me]

    def hidden_sends(k, ready, lo=0, hi=4):
        first = plane(k) * 4

        @pl.loop(lo, hi)
        def _(i):
            e = first + i

            @pl.when((e != me) & ready)
            def _():
                h_copy(e).start()

    def place_waits():
        @pl.loop(1, n_ep)
        def _(d):
            s = lax.rem(me + d, n_ep)
            remote(table.at[s], place_all.at[s], pl_send.at[d], pl_recv.at[s], ep=s).wait_recv()

    def w_waits():
        for d in range(1, n_rep):
            q = lax.rem(rep + d, n_rep)
            remote(w_ref, wfull.at[q], w_send.at[d], w_recv.at[q], rep=q).wait_recv()

    def held(k):
        return jnp.logical_not(gateway) & (spot(k) >= half)

    def returns(k, straight, free):
        first = plane(k) * 4 + 2 * (y if straight else 1 - y)

        @pl.loop(0, 2)
        def _(i):
            s = first + i

            @pl.when((s != me) & free)
            def _():
                r_copy(s).start()

    def group(k):
        first = plane(k) * 4
        og_wait(first + 1 - c)
        og_wait(first + 3 - c)

        @pl.loop(0, 4)
        def _(i):
            s = first + i
            info = place_all[s]
            ids = lax.broadcasted_iota(jnp.int32, (cap, tok), 0).astype(jnp.float32)
            pick = jnp.where(ids == info[0:1, :], 1.0, 0.0)
            factor = jnp.sum(pick * info[1:2, :], axis=1, keepdims=True)
            got = factor * jnp.dot(
                pick.astype(jnp.bfloat16), og_all[s], preferred_element_type=jnp.float32
            )
            rows[pl.ds(pl.multiple_of(s * cap, 16), cap), :] = got.astype(jnp.bfloat16)

        here = rows[pl.ds(pl.multiple_of(first * cap, 16), 4 * cap), :]
        got = lax.dot_general(
            here,
            wfull[...].reshape(inner, width),
            (((1,), (1,)), ((), ())),
            preferred_element_type=jnp.float32,
        )
        igbuf[pl.ds(first, 4)] = got.astype(jnp.bfloat16).reshape(4, cap, inner)

    with scope("hid_dma"):
        own_hidden.wait()
    last = outer - 1
    turn_k = min(2, last)
    inner_end = jnp.logical_not(gateway)

    def far(k):
        return spot(k) >= half

    def adjacent(k):
        return spot(k) == half

    def early(k):
        return (adjacent(k) & gateway) | (jnp.logical_not(far(k)) & inner_end)

    for k in [*range(1, last), 0, last]:
        with scope(f"hid{k}"):
            hidden_group(k)
        if k == 1:
            hidden_sends(k, early(k), 0, 2)

            @pl.when(inner_end)
            def _():
                own_across(start)

            hidden_sends(k, early(k), 2, 4)
        else:
            hidden_sends(k, k == 0 or early(k))
    for k in range(1, outer):
        with scope(f"relay{k}"):
            relay(k, start, True)
        if k == 1:
            for i in range(1, outer):
                hidden_sends(i, jnp.logical_not(far(i)) & gateway)
            with scope("cross0"):
                crossing(0, start, True)
        if k == turn_k:
            for i in range(1, outer):
                hidden_sends(i, adjacent(i) & inner_end)
    with scope("cross1"):
        crossing(1, start, True)
    with scope("w_wait"):
        place_waits()
        own_og.wait()
        own_w.wait()
        w_waits()
    def beyond(who):
        for k in range(1, outer):
            hidden_sends(k, far(k) & jnp.logical_not(adjacent(k)) & who)

    beyond(inner_end)
    with scope("group0"):
        group(0)
    with scope("group1"):
        group(1)
    beyond(gateway)
    for k in range(2, outer):
        if k == last:
            for i in range(last):
                returns(i, True, jnp.logical_not(held(i)))
        with scope(f"cross{k}"):
            crossing(k, start, True)
        with scope(f"group{k}"):
            group(k)
    returns(last, True, jnp.logical_not(held(last)))

    own = pltpu.make_async_copy(
        igbuf.at[me, pl.ds(0, sent)], back.at[me, pl.ds(0, sent)], r_recv.at[me]
    )
    own.start()

    with scope("h_wait"):
        @pl.loop(1, n_ep)
        def _(d):
            s = lax.rem(me + d, n_ep)
            remote(hsend.at[s, pl.ds(0, sent)], hrecv.at[s, pl.ds(0, sent)], h_send.at[s], h_recv.at[s], ep=s).wait_recv()
    for k in range(1, outer):
        returns(k, True, held(k))

    def g_copy(d, j, q, slot):
        cols = pl.ds(j * wide, wide)
        return remote(
            term.at[q, :, cols], parts.at[slot, :, cols],
            g_send.at[d, j], g_recv.at[slot, j], rep=q,
        )

    left = hrecv[...].reshape(n_ep * cap, inner)
    for j in range(chunks):
        cols = pl.ds(j * wide, wide)
        with scope(f"grad{j}"):
            got = lax.dot_general(
                left, rows[:, cols], (((0,), (0,)), ((), ())), preferred_element_type=jnp.float32
            )
            term[:, :, cols] = got.astype(jnp.bfloat16).reshape(n_rep, own_rows, wide)
        for d in range(1, n_rep):
            g_copy(d, j, lax.rem(rep + d, n_rep), rep).start()

    for k in range(outer):
        returns(k, False, True)

    def collect(j):
        p = lax.rem(near + j, half) if j < half else outer - 1 - (j - half)
        first = real(p) * 4

        with scope(f"rwait{j}"):
            @pl.loop(0, 4)
            def _(i):
                s = first + i

                @pl.when(s != me)
                def _():
                    remote(
                        igbuf.at[s, pl.ds(0, sent)], back.at[s, pl.ds(0, sent)],
                        r_send.at[s], r_recv.at[s], ep=s,
                    ).wait_recv()

        with scope(f"collect{j}"):
            got = lax.dot_general(
                slot_pick(first),
                back[pl.ds(first, 4)].reshape(4 * cap, inner),
                (((0,), (0,)), ((), ())),
                preferred_element_type=jnp.float32,
            ).astype(jnp.bfloat16)
            out_ref[...] = got if j == 0 else out_ref[...] + got

    own.wait()
    for j in range(outer):
        collect(j)

    total = jnp.zeros((own_rows, 1), jnp.float32)
    for j in range(chunks):
        cols = pl.ds(j * wide, wide)
        part = term[rep, :, cols].astype(jnp.float32)
        for d in range(1, n_rep):
            q = lax.rem(rep + d, n_rep)
            with scope(f"gwait{j}"):
                g_copy(d, j, q, q).wait_recv()
            part = part + parts[q, :, cols].astype(jnp.float32)
        grad[:, cols] = part
        square = part * part
        total = total + jnp.sum(square, axis=1, keepdims=True)
        coln_ref[:, cols] = decay_rate * colm_ref[:, cols] + (1.0 - decay_rate) * (
            jnp.sum(square, axis=0, keepdims=True) / own_rows + epsilon
        )
    diagonal = lax.broadcasted_iota(jnp.int32, (own_rows, own_rows), 0) == (
        lax.broadcasted_iota(jnp.int32, (own_rows, own_rows), 1)
    )
    rowm = jnp.sum(jnp.where(diagonal, rowm_ref[...], 0.0), axis=1, keepdims=True)
    row_new = decay_rate * rowm + (1.0 - decay_rate) * (total / width + epsilon)
    rown_ref[...] = jnp.sum(jnp.where(diagonal, row_new, 0.0), axis=0, keepdims=True)
    mean = jnp.sum(row_new, axis=0, keepdims=True) / own_rows
    for j in range(chunks):
        cols = pl.ds(j * wide, wide)
        second = row_new * coln_ref[:, cols] / mean
        with scope(f"update{j}"):
            update_ref[:, cols] = (grad[:, cols] * lax.rsqrt(second)).astype(jnp.bfloat16)

    @pl.loop(1, n_ep)
    def _(d):
        s = lax.rem(me + d, n_ep)
        place_copy(d).wait_send()
        h_copy(s).wait_send()
        r_copy(s).wait_send()

    own_sends(finish)
    own_across(finish)
    crossing(0, finish, False)
    for k in range(1, outer):
        relay(k, finish, False)
        crossing(k, finish, False)
    for copy in w_copies:
        copy.wait_send()
    for j in range(chunks):
        for d in range(1, n_rep):
            g_copy(d, j, lax.rem(rep + d, n_rep), rep).wait_send()


def local(out_grad, hidden, expert_ids, gates, weights, row_moment, col_moment):
    tok, top = expert_ids.shape
    width = out_grad.shape[1]
    inner = hidden.shape[2]
    n_ep, n_rep = lax.axis_size("ep"), lax.axis_size("rep")
    capacity = max(2, tok * top * 9 // (8 * n_ep))
    sent, cap = up_to(capacity, 8), up_to(capacity, 16)
    outer = n_ep // 4
    own_rows = inner // n_rep
    routes = tok * top
    chunks = 4

    vmem = pl.BlockSpec(memory_space=pltpu.VMEM)
    anywhere = pl.BlockSpec(memory_space=pl.ANY)
    dma = pltpu.SemaphoreType.DMA
    hidden_grad, update, row_new, col_new = pl.pallas_call(
        functools.partial(kernel, (n_ep, n_rep, outer, sent, cap, chunks)),
        out_shape=(
            jax.ShapeDtypeStruct((routes, inner), jnp.bfloat16),
            jax.ShapeDtypeStruct((own_rows, width), jnp.bfloat16),
            jax.ShapeDtypeStruct((1, own_rows), jnp.float32),
            jax.ShapeDtypeStruct((1, width), jnp.float32),
        ),
        in_specs=[anywhere, anywhere, vmem, vmem, anywhere, vmem, vmem],
        out_specs=(vmem, vmem, vmem, vmem),
        scratch_shapes=[
            pltpu.VMEM((n_ep, tok, width), jnp.bfloat16),
            pltpu.VMEM((1, routes), jnp.float32),
            pltpu.VMEM((n_ep, 8, tok), jnp.float32),
            pltpu.VMEM((n_ep, 8, tok), jnp.float32),
            pltpu.VMEM((n_ep, cap, inner), jnp.bfloat16),
            pltpu.VMEM((n_ep, cap, inner), jnp.bfloat16),
            pltpu.VMEM((n_ep * cap, width), jnp.bfloat16),
            pltpu.VMEM((n_ep, cap, inner), jnp.bfloat16),
            pltpu.VMEM((n_ep, cap, inner), jnp.bfloat16),
            pltpu.VMEM((n_rep, own_rows, width), jnp.bfloat16),
            pltpu.VMEM((n_rep, own_rows, width), jnp.bfloat16),
            pltpu.VMEM((own_rows, width), jnp.float32),
            dma((n_ep,)),
            dma((outer // 2,)),
            dma((outer * (outer // 2),)),
            dma((outer,)),
            dma((2 * outer,)),
            dma((n_ep,)),
            dma((n_ep,)),
            dma((n_ep,)),
            dma((n_ep,)),
            dma((n_ep,)),
            dma((n_ep,)),
            dma((n_rep,)),
            dma((n_rep,)),
            dma((n_rep, chunks)),
            dma((n_rep, chunks)),
            dma((3,)),
        ],
        compiler_params=pltpu.CompilerParams(
            collective_id=0, has_side_effects=True, vmem_limit_bytes=67043328
        ),
    )(
        out_grad,
        hidden.reshape(routes, inner),
        expert_ids.T,
        gates.T,
        weights[0],
        row_moment.reshape(1, own_rows),
        col_moment.reshape(1, width),
    )

    return (
        hidden_grad.reshape(tok, top, inner),
        update[None],
        row_new.reshape(1, own_rows),
        col_new.reshape(1, 1, width),
    )


def solution(mesh):
    return jax.shard_map(
        local,
        mesh=mesh,
        in_specs=(
            P(("ep", "rep"), None),
            P(("ep", "rep"), None, None),
            P(("ep", "rep"), None),
            P(("ep", "rep"), None),
            P("ep", "rep", None),
            P("ep", "rep"),
            P("ep", "rep", None),
        ),
        out_specs=(
            P(("ep", "rep"), None, None),
            P("ep", "rep", None),
            P("ep", "rep"),
            P("ep", "rep", None),
        ),
        check_vma=False,
    )
```

time: 137 us -> 126 us (0.920)
  the two profiles are of different devices: /device:TPU:29 before, /device:TPU:1 now
where the time goes in v1:
time: 126 us
  Pallas kernels  120 us (95%)
  local copies, waits for them, and re-layouts  5.08 us (4%)
    pallas_call x1, Pallas kernels, local(): pl.pallas_call(functools.partial(kernel, (n_ep, n_rep, outer, sent, cap,...  120 us
    unnamed x10, local copies, waits for them, and re-layouts  5.08 us

profile of v1, /device:TPU:1, one launch (start us, length us, event | category | flops | bytes accessed | tf_op | source)
XLA Modules:
  0.0 125.9 jit_solution(14467831105859331055)
XLA Ops:
  0.6 120.1 %shard_map.102 = (bf16[1024,768]{1,0:T(8,128)(2,1)}, bf16[384,2048]{1,0:T(8,128)(2,1)}, f32[1,384]{1,0:T(1,128)}, f32[1,2048]{1,0:T(1,128)}) custom-call(bf16[128,2048]{1,0:T(8,128)(2,1)} %og_ref.1, bf16[1024,768]{1,0:T(8,128)(2,1)} %bitcast.8, s32[8,128]{1,0:T(8,128)} %bitcast.14, f32[8,128]{1,0:T(8,128)} %bitcast.15, bf16[384,2048]{1,0:T(8,128)(2,1)} %bitcast.9, ...), custom_call_target="tpu_custom_call" | custom-call | tf_op jit(solution)/shard_map/pallas_call | solution.py:485
  120.8 0.0 copy-start
  120.8 2.8 %copy.15 = bf16[128,8,768]{2,1,0:T(8,128)(2,1)} copy(bf16[128,8,768]{2,1,0:T(8,128)(2,1)} %bitcast.11) | data formatting | bytes 3145728
  123.5 0.0 copy-done
  123.6 0.0 copy-start.2
  123.6 0.0 copy-start.1
  123.6 1.1 copy.16
  124.7 0.0 copy-done.2
  124.7 0.6 copy.17
  125.3 0.0 copy-done.1
  125.3 0.6 copy.18
Async XLA Ops:
  120.8 2.8 %copy-start = (bf16[384,2048]{1,0:T(8,128)(2,1)S(1)}, bf16[384,2048]{1,0:T(8,128)(2,1)}, u32[]{:S(2)}) copy-start(bf16[384,2048]{1,0:T(8,128)(2,1)} %get-tuple-element.9) | copy-start | bytes 4718596
  123.6 1.1 copy-start.2
  123.6 1.7 %copy-start.1 = (f32[1,2048]{1,0:T(1,128)S(1)}, f32[1,2048]{1,0:T(1,128)}, u32[]{:S(2)}) copy-start(f32[1,2048]{1,0:T(1,128)} %get-tuple-element.11) | copy-start | bytes 24580

commit v2 on v1

--- a/solution.py
+++ b/solution.py
@@ -24,12 +24,9 @@
     ids_ref,
     gates_ref,
     w_ref,
-    rowm_ref,
-    colm_ref,
+    result_ref,
+    parts,
     out_ref,
-    update_ref,
-    rown_ref,
-    coln_ref,
     og_all,
     slot,
     table,
@@ -40,8 +37,7 @@
     igbuf,
     back,
     wfull,
-    parts,
-    grad,
+    term,
     og_recv,
     own_sem,
     relay_sem,
@@ -65,7 +61,6 @@
     top = routes // tok
     own_rows = inner // n_rep
     wide = width // chunks
-    term = wfull
     me = lax.axis_index("ep")
     rep = lax.axis_index("rep")
     z, y, c = me // 4, (me // 2) % 2, me % 2
@@ -264,7 +259,7 @@
             def _():
                 r_copy(s).start()
 
-    def group(k):
+    def gather(k):
         first = plane(k) * 4
         og_wait(first + 1 - c)
         og_wait(first + 3 - c)
@@ -281,6 +276,8 @@
             )
             rows[pl.ds(pl.multiple_of(s * cap, 16), cap), :] = got.astype(jnp.bfloat16)
 
+    def product(k):
+        first = plane(k) * 4
         here = rows[pl.ds(pl.multiple_of(first * cap, 16), 4 * cap), :]
         got = lax.dot_general(
             here,
@@ -289,6 +286,10 @@
             preferred_element_type=jnp.float32,
         )
         igbuf[pl.ds(first, 4)] = got.astype(jnp.bfloat16).reshape(4, cap, inner)
+
+    def group(k):
+        gather(k)
+        product(k)
 
     with scope("hid_dma"):
         own_hidden.wait()
@@ -353,21 +354,20 @@
         with scope(f"cross{k}"):
             crossing(k, start, True)
         with scope(f"group{k}"):
-            group(k)
-    returns(last, True, jnp.logical_not(held(last)))
-
-    own = pltpu.make_async_copy(
-        igbuf.at[me, pl.ds(0, sent)], back.at[me, pl.ds(0, sent)], r_recv.at[me]
-    )
-    own.start()
+            if k < last:
+                group(k)
+            else:
+                gather(k)
 
     with scope("h_wait"):
         @pl.loop(1, n_ep)
         def _(d):
             s = lax.rem(me + d, n_ep)
             remote(hsend.at[s, pl.ds(0, sent)], hrecv.at[s, pl.ds(0, sent)], h_send.at[s], h_recv.at[s], ep=s).wait_recv()
-    for k in range(1, outer):
+    for k in range(1, last):
         returns(k, True, held(k))
+    for k in range(last):
+        returns(k, False, True)
 
     def g_copy(d, j, q, slot):
         cols = pl.ds(j * wide, wide)
@@ -386,9 +386,18 @@
             term[:, :, cols] = got.astype(jnp.bfloat16).reshape(n_rep, own_rows, wide)
         for d in range(1, n_rep):
             g_copy(d, j, lax.rem(rep + d, n_rep), rep).start()
-
-    for k in range(outer):
-        returns(k, False, True)
+        if j == 0:
+            with scope("product"):
+                product(last)
+            returns(last, True, True)
+            returns(last, False, True)
+            own = pltpu.make_async_copy(
+                igbuf.at[me, pl.ds(0, sent)], back.at[me, pl.ds(0, sent)], r_recv.at[me]
+            )
+            own.start()
+
+    kept = pltpu.make_async_copy(term.at[rep], parts.at[rep], l_sem.at[0])
+    kept.start()
 
     def collect(j):
         p = lax.rem(near + j, half) if j < half else outer - 1 - (j - half)
@@ -419,34 +428,8 @@
     for j in range(outer):
         collect(j)
 
-    total = jnp.zeros((own_rows, 1), jnp.float32)
-    for j in range(chunks):
-        cols = pl.ds(j * wide, wide)
-        part = term[rep, :, cols].astype(jnp.float32)
-        for d in range(1, n_rep):
-            q = lax.rem(rep + d, n_rep)
-            with scope(f"gwait{j}"):
-                g_copy(d, j, q, q).wait_recv()
-            part = part + parts[q, :, cols].astype(jnp.float32)
-        grad[:, cols] = part
-        square = part * part
-        total = total + jnp.sum(square, axis=1, keepdims=True)
-        coln_ref[:, cols] = decay_rate * colm_ref[:, cols] + (1.0 - decay_rate) * (
-            jnp.sum(square, axis=0, keepdims=True) / own_rows + epsilon
-        )
-    diagonal = lax.broadcasted_iota(jnp.int32, (own_rows, own_rows), 0) == (
-        lax.broadcasted_iota(jnp.int32, (own_rows, own_rows), 1)
-    )
-    rowm = jnp.sum(jnp.where(diagonal, rowm_ref[...], 0.0), axis=1, keepdims=True)
-    row_new = decay_rate * rowm + (1.0 - decay_rate) * (total / width + epsilon)
-    rown_ref[...] = jnp.sum(jnp.where(diagonal, row_new, 0.0), axis=0, keepdims=True)
-    mean = jnp.sum(row_new, axis=0, keepdims=True) / own_rows
-    for j in range(chunks):
-        cols = pl.ds(j * wide, wide)
-        second = row_new * coln_ref[:, cols] / mean
-        with scope(f"update{j}"):
-            update_ref[:, cols] = (grad[:, cols] * lax.rsqrt(second)).astype(jnp.bfloat16)
-
+    result = pltpu.make_async_copy(out_ref, result_ref, l_sem.at[1])
+    result.start()
     @pl.loop(1, n_ep)
     def _(d):
         s = lax.rem(me + d, n_ep)
@@ -465,6 +448,95 @@
     for j in range(chunks):
         for d in range(1, n_rep):
             g_copy(d, j, lax.rem(rep + d, n_rep), rep).wait_send()
+    kept.wait()
+    result.wait()
+    for j in range(chunks):
+        for d in range(1, n_rep):
+            q = lax.rem(rep + d, n_rep)
+            with scope(f"gwait{j}"):
+                g_copy(d, j, q, q).wait_recv()
+
+
+def finish_kernel(
+    dims,
+    result_ref,
+    parts_ref,
+    rowm_ref,
+    colm_ref,
+    out_ref,
+    update_ref,
+    rown_ref,
+    coln_ref,
+    result,
+    parts,
+    grad,
+    update,
+    in_sem,
+    part_sem,
+    out_sem,
+    update_sem,
+):
+    pieces, chunks = dims
+    n_rep, own_rows, width = parts.shape
+    wide = width // chunks
+    tall = result.shape[0] // pieces
+
+    def load(j):
+        cols = pl.ds(j * wide, wide)
+        return pltpu.make_async_copy(parts_ref.at[:, :, cols], parts.at[:, :, cols], part_sem.at[j])
+
+    def take(i):
+        span = pl.ds(i * tall, tall)
+        return pltpu.make_async_copy(result_ref.at[span], result.at[span], in_sem.at[i])
+
+    def give(i):
+        span = pl.ds(i * tall, tall)
+        return pltpu.make_async_copy(result.at[span], out_ref.at[span], out_sem.at[i])
+
+    def put(j):
+        cols = pl.ds(j * wide, wide)
+        return pltpu.make_async_copy(update.at[:, cols], update_ref.at[:, cols], update_sem.at[j])
+
+    for j in range(max(chunks, pieces)):
+        if j < chunks:
+            load(j).start()
+        if j < pieces:
+            take(j).start()
+    diagonal = lax.broadcasted_iota(jnp.int32, (own_rows, own_rows), 0) == (
+        lax.broadcasted_iota(jnp.int32, (own_rows, own_rows), 1)
+    )
+    rowm = jnp.sum(jnp.where(diagonal, rowm_ref[...], 0.0), axis=1, keepdims=True)
+    total = jnp.zeros((own_rows, 1), jnp.float32)
+    for j in range(chunks):
+        cols = pl.ds(j * wide, wide)
+        load(j).wait()
+        part = parts[0, :, cols].astype(jnp.float32)
+        for q in range(1, n_rep):
+            part = part + parts[q, :, cols].astype(jnp.float32)
+        grad[:, cols] = part
+        square = part * part
+        total = total + jnp.sum(square, axis=1, keepdims=True)
+        coln_ref[:, cols] = decay_rate * colm_ref[:, cols] + (1.0 - decay_rate) * (
+            jnp.sum(square, axis=0, keepdims=True) / own_rows + epsilon
+        )
+        if j < pieces:
+            take(j).wait()
+            give(j).start()
+    for i in range(chunks, pieces):
+        take(i).wait()
+        give(i).start()
+    row_new = decay_rate * rowm + (1.0 - decay_rate) * (total / width + epsilon)
+    rown_ref[...] = jnp.sum(jnp.where(diagonal, row_new, 0.0), axis=0, keepdims=True)
+    mean = jnp.sum(row_new, axis=0, keepdims=True) / own_rows
+    for j in range(chunks):
+        cols = pl.ds(j * wide, wide)
+        second = row_new * coln_ref[:, cols] / mean
+        update[:, cols] = (grad[:, cols] * lax.rsqrt(second)).astype(jnp.bfloat16)
+        put(j).start()
+    for i in range(pieces):
+        give(i).wait()
+    for j in range(chunks):
+        put(j).wait()
 
 
 def local(out_grad, hidden, expert_ids, gates, weights, row_moment, col_moment):
@@ -482,17 +554,16 @@
     vmem = pl.BlockSpec(memory_space=pltpu.VMEM)
     anywhere = pl.BlockSpec(memory_space=pl.ANY)
     dma = pltpu.SemaphoreType.DMA
-    hidden_grad, update, row_new, col_new = pl.pallas_call(
+    result, parts = pl.pallas_call(
         functools.partial(kernel, (n_ep, n_rep, outer, sent, cap, chunks)),
         out_shape=(
             jax.ShapeDtypeStruct((routes, inner), jnp.bfloat16),
-            jax.ShapeDtypeStruct((own_rows, width), jnp.bfloat16),
-            jax.ShapeDtypeStruct((1, own_rows), jnp.float32),
-            jax.ShapeDtypeStruct((1, width), jnp.float32),
+            jax.ShapeDtypeStruct((n_rep, own_rows, width), jnp.bfloat16),
         ),
-        in_specs=[anywhere, anywhere, vmem, vmem, anywhere, vmem, vmem],
-        out_specs=(vmem, vmem, vmem, vmem),
+        in_specs=[anywhere, anywhere, vmem, vmem, anywhere],
+        out_specs=(anywhere, anywhere),
         scratch_shapes=[
+            pltpu.VMEM((routes, inner), jnp.bfloat16),
             pltpu.VMEM((n_ep, tok, width), jnp.bfloat16),
             pltpu.VMEM((1, routes), jnp.float32),
             pltpu.VMEM((n_ep, 8, tok), jnp.float32),
@@ -504,7 +575,6 @@
             pltpu.VMEM((n_ep, cap, inner), jnp.bfloat16),
             pltpu.VMEM((n_rep, own_rows, width), jnp.bfloat16),
             pltpu.VMEM((n_rep, own_rows, width), jnp.bfloat16),
-            pltpu.VMEM((own_rows, width), jnp.float32),
             dma((n_ep,)),
             dma((outer // 2,)),
             dma((outer * (outer // 2),)),
@@ -531,9 +601,30 @@
         expert_ids.T,
         gates.T,
         weights[0],
-        row_moment.reshape(1, own_rows),
-        col_moment.reshape(1, width),
     )
+    pieces, blocks = 4, 4
+    hidden_grad, update, row_new, col_new = pl.pallas_call(
+        functools.partial(finish_kernel, (pieces, blocks)),
+        out_shape=(
+            jax.ShapeDtypeStruct((routes, inner), jnp.bfloat16),
+            jax.ShapeDtypeStruct((own_rows, width), jnp.bfloat16),
+            jax.ShapeDtypeStruct((1, own_rows), jnp.float32),
+            jax.ShapeDtypeStruct((1, width), jnp.float32),
+        ),
+        in_specs=[anywhere, anywhere, vmem, vmem],
+        out_specs=(anywhere, anywhere, vmem, vmem),
+        scratch_shapes=[
+            pltpu.VMEM((routes, inner), jnp.bfloat16),
+            pltpu.VMEM((n_rep, own_rows, width), jnp.bfloat16),
+            pltpu.VMEM((own_rows, width), jnp.float32),
+            pltpu.VMEM((own_rows, width), jnp.bfloat16),
+            dma((pieces,)),
+            dma((blocks,)),
+            dma((pieces,)),
+            dma((blocks,)),
+        ],
+        compiler_params=pltpu.CompilerParams(vmem_limit_bytes=67043328),
+    )(result, parts, row_moment.reshape(1, own_rows), col_moment.reshape(1, width))
 
     return (
         hidden_grad.reshape(tok, top, inner),

time: 126 us -> 123 us (0.976)
  local copies, waits for them, and re-layouts: 5.08 us -> 0 us
  Pallas kernels: 120 us -> 122 us
    pallas_call x0 -> x1, Pallas kernels: none -> 5.24 us  [local(): pl.pallas_call(functools.partial(finish_kernel, (pieces, blocks)), out_sh...]
    unnamed x10 -> x0, local copies, waits for them, and re-layouts: 5.08 us -> none
    pallas_call x1, Pallas kernels: 120 us -> 117 us  [local(): pl.pallas_call(functools.partial(kernel, (n_ep, n_rep, outer, sent, cap,...]
where the time goes in v2:
time: 123 us
  Pallas kernels  122 us (99%)
    pallas_call x1, Pallas kernels, local(): pl.pallas_call(functools.partial(kernel, (n_ep, n_rep, outer, sent, cap,...  117 us
    pallas_call x1, Pallas kernels, local(): pl.pallas_call(functools.partial(finish_kernel, (pieces, blocks)), out_sh...  5.24 us

profile of v2, /device:TPU:1, one launch (start us, length us, event | category | flops | bytes accessed | tf_op | source)
XLA Modules:
  0.0 122.8 jit_solution(463438212281040879)
XLA Ops:
  0.6 116.7 %shard_map.102 = (bf16[1024,768]{1,0:T(8,128)(2,1)}, bf16[2,384,2048]{2,1,0:T(8,128)(2,1)}) custom-call(bf16[128,2048]{1,0:T(8,128)(2,1)} %og_ref.1, bf16[1024,768]{1,0:T(8,128)(2,1)} %bitcast.8, s32[8,128]{1,0:T(8,128)} %bitcast.11, f32[8,128]{1,0:T(8,128)} %bitcast.12, bf16[384,2048]{1,0:T(8,128)(2,1)} %bitcast.9), custom_call_target="tpu_custom_call" | custom-call | tf_op jit(solution)/shard_map/pallas_call | solution.py:557
  117.4 5.2 %shard_map.103 = (bf16[1024,768]{1,0:T(8,128)(2,1)}, bf16[384,2048]{1,0:T(8,128)(2,1)}, f32[1,384]{1,0:T(1,128)}, f32[1,2048]{1,0:T(1,128)}) custom-call(bf16[1024,768]{1,0:T(8,128)(2,1)} %get-tuple-element.10.result_ref, bf16[2,384,2048]{2,1,0:T(8,128)(2,1)} %get-tuple-element.11.parts_ref, f32[1,384]{1,0:T(1,128)} %rowm_ref.1, f32[1,2048]{1,0:T(1,128)} %bitcast.10), custom_call_target="tpu_custom_call" | custom-call | tf_op jit(solution)/shard_map/pallas_call | solution.py:606

commit v3 on v2

--- a/solution.py
+++ b/solution.py
@@ -54,6 +54,7 @@
     g_send,
     g_recv,
     l_sem,
+    result_sem,
 ):
     n_ep, n_rep, outer, sent, cap, chunks = dims
     tok, width = og_ref.shape
@@ -399,6 +400,13 @@
     kept = pltpu.make_async_copy(term.at[rep], parts.at[rep], l_sem.at[0])
     kept.start()
 
+    pieces = 4
+    tall = routes // pieces
+
+    def result(i):
+        span = pl.ds(i * tall, tall)
+        return pltpu.make_async_copy(out_ref.at[span], result_ref.at[span], result_sem.at[i])
+
     def collect(j):
         p = lax.rem(near + j, half) if j < half else outer - 1 - (j - half)
         first = real(p) * 4
@@ -414,6 +422,21 @@
                         igbuf.at[s, pl.ds(0, sent)], back.at[s, pl.ds(0, sent)],
                         r_send.at[s], r_recv.at[s], ep=s,
                     ).wait_recv()
+
+        if j == last:
+            for i in range(pieces):
+                span = pl.ds(i * tall, tall)
+                ids = lax.broadcasted_iota(jnp.int32, (4 * cap, tall), 0) + first * cap
+                pick = jnp.where(ids.astype(jnp.float32) == slot[:, span], 1.0, 0.0)
+                got = lax.dot_general(
+                    pick.astype(jnp.bfloat16),
+                    back[pl.ds(first, 4)].reshape(4 * cap, inner),
+                    (((0,), (0,)), ((), ())),
+                    preferred_element_type=jnp.float32,
+                ).astype(jnp.bfloat16)
+                out_ref[span, :] = out_ref[span, :] + got
+                result(i).start()
+            return
 
         with scope(f"collect{j}"):
             got = lax.dot_general(
@@ -428,8 +451,6 @@
     for j in range(outer):
         collect(j)
 
-    result = pltpu.make_async_copy(out_ref, result_ref, l_sem.at[1])
-    result.start()
     @pl.loop(1, n_ep)
     def _(d):
         s = lax.rem(me + d, n_ep)
@@ -449,7 +470,8 @@
         for d in range(1, n_rep):
             g_copy(d, j, lax.rem(rep + d, n_rep), rep).wait_send()
     kept.wait()
-    result.wait()
+    for i in range(pieces):
+        result(i).wait()
     for j in range(chunks):
         for d in range(1, n_rep):
             q = lax.rem(rep + d, n_rep)
@@ -591,6 +613,7 @@
             dma((n_rep, chunks)),
             dma((n_rep, chunks)),
             dma((3,)),
+            dma((4,)),
         ],
         compiler_params=pltpu.CompilerParams(
             collective_id=0, has_side_effects=True, vmem_limit_bytes=67043328

time: 123 us -> 122 us (level)
  no operation moved by 1% of the time
where the time goes in v3:
time: 122 us
  Pallas kernels  121 us (99%)
    pallas_call x1, Pallas kernels, local(): pl.pallas_call(functools.partial(kernel, (n_ep, n_rep, outer, sent, cap,...  116 us
    pallas_call x1, Pallas kernels, local(): pl.pallas_call(functools.partial(finish_kernel, (pieces, blocks)), out_sh...  5.24 us

profile of v3, /device:TPU:1, one launch (start us, length us, event | category | flops | bytes accessed | tf_op | source)
XLA Modules:
  0.0 122.1 jit_solution(2733928652493506447)
XLA Ops:
  0.6 116.1 %shard_map.102 = (bf16[1024,768]{1,0:T(8,128)(2,1)}, bf16[2,384,2048]{2,1,0:T(8,128)(2,1)}) custom-call(bf16[128,2048]{1,0:T(8,128)(2,1)} %og_ref.1, bf16[1024,768]{1,0:T(8,128)(2,1)} %bitcast.8, s32[8,128]{1,0:T(8,128)} %bitcast.11, f32[8,128]{1,0:T(8,128)} %bitcast.12, bf16[384,2048]{1,0:T(8,128)(2,1)} %bitcast.9), custom_call_target="tpu_custom_call" | custom-call | tf_op jit(solution)/shard_map/pallas_call | solution.py:579
  116.7 5.2 %shard_map.103 = (bf16[1024,768]{1,0:T(8,128)(2,1)}, bf16[384,2048]{1,0:T(8,128)(2,1)}, f32[1,384]{1,0:T(1,128)}, f32[1,2048]{1,0:T(1,128)}) custom-call(bf16[1024,768]{1,0:T(8,128)(2,1)} %get-tuple-element.10.result_ref, bf16[2,384,2048]{2,1,0:T(8,128)(2,1)} %get-tuple-element.11.parts_ref, f32[1,384]{1,0:T(1,128)} %rowm_ref.1, f32[1,2048]{1,0:T(1,128)} %bitcast.10), custom_call_target="tpu_custom_call" | custom-call | tf_op jit(solution)/shard_map/pallas_call | solution.py:629
